TPU v7x, 32 devices: a whole 2x2x4 slice. The times are simulated.
32 devices in a mesh: ctx: 4 (over y, x), tp: 4 (over z), grp: 2 (over core).
Axes of the slice: x: 2, y: 2, z: 4, core: 2. Of those that a mesh axis runs over, the one named last changes fastest.
Arguments:
- patches: bfloat16 [32, 5120], P('ctx'), may hold values from -6 to 6
- route_count: int32 [4, 4], replicated, may hold values from 0 to 2, as said below
- text_states: bfloat16 [512, 4096], P('ctx', ('tp', 'grp')), may hold values from -6 to 6
- segment_ids: int32 [512], replicated, may hold values from 0 to 3, never falling along the last dimension, each value on 1 to 256 neighbouring positions
- vision_gain: float32 [1280], replicated, may hold values from 0.1 to 1.9
- merge_up: bfloat16 [5120, 2560], P(None, ('tp', 'grp')), may hold values from -0.078125 to 0.078125
- merge_down: bfloat16 [2560, 4096], P(('tp', 'grp')), may hold values from -0.125 to 0.125
- norm_gain: float32 [4096], replicated, may hold values from 0.1 to 1.9
- query_weight: bfloat16 [4096, 4096], P(None, ('tp', 'grp')), may hold values from -0.62928387 to 0.62928387
- kv_weight: bfloat16 [4096, 2048], P(None, 'tp'), may hold values from -0.4578688 to 0.4578688
Outputs:
- attended: bfloat16 [512, 4096], P('ctx', ('tp', 'grp'))
Inputs may be any that keep to these rules, and one draw needn't show every extreme that they name: route_count[c, d] counts the live rows among the 2 rows that source c holds for owner d; at least one owner gets 2 live rows from every source. `segment_ids`: never falling along the packed batch; a segment has at most 256 positions.
All inputs are finite; a program needn't handle non-finite values.
Results may differ from a plain program's by a relative error of at most 0.04.
Values may be sent and summed in bfloat16 or wider, within the bound.
A program may use at most 64 MiB of HBM per device.

v0:
```python
import jax
import jax.numpy as jnp
from jax import lax
from jax.sharding import PartitionSpec as P

HQ = 32
KVH = 8
HD = 128
EPSILON = 1e-06
NEGATIVE = -1e30


def rms_scale(values, gain):
    mean_square = jnp.mean(values * values, axis=-1, keepdims=True)
    return values * lax.rsqrt(mean_square + EPSILON) * gain


def attend(
    running,
    queries4,
    shard_piece,
    key_pos,
    query_pos,
    query_seg,
    segment_ids,
    visual_count,
    tokens_dev,
):
    weighted, running_max, denominator = running
    piece_rows = shard_piece.shape[0]
    kv_heads = queries4.shape[1]
    kv_split = shard_piece.reshape(piece_rows, kv_heads, 2, HD)
    key_block = kv_split[:, :, 0]
    value_block = kv_split[:, :, 1]
    key_owner = key_pos // tokens_dev
    owner_match = key_owner[:, None] == jnp.arange(visual_count.shape[0], dtype=jnp.int32)[None, :]
    visual_limit = jnp.sum(jnp.where(owner_match, visual_count[None, :], 0), axis=1)
    key_visual = key_pos % tokens_dev < visual_limit
    key_seg = segment_ids[key_pos]
    allowed = (query_seg[:, None] == key_seg[None, :]) & (
        key_visual[None, :] | (key_pos[None, :] <= query_pos[:, None])
    )
    scores = jnp.where(
        allowed,
        jnp.einsum("qkgd,rkd->kgqr", queries4, key_block, preferred_element_type=jnp.float32)
        * HD ** (-0.5),
        NEGATIVE,
    )
    new_max = jnp.maximum(running_max, jnp.max(scores, axis=-1))
    weights = jnp.exp(jnp.where(allowed, scores - new_max[..., None], NEGATIVE))
    denominator = jnp.sum(weights, axis=-1)
    weighted = jnp.einsum(
        "kgqr,rkd->kgqd",
        weights.astype(jnp.bfloat16),
        value_block,
        preferred_element_type=jnp.float32,
    )
    return (weighted, new_max, denominator)


def start_state(kv_heads, per_head, tokens_dev):
    return (
        jnp.zeros((kv_heads, per_head, tokens_dev, HD), jnp.float32),
        jnp.full((kv_heads, per_head, tokens_dev), NEGATIVE, jnp.float32),
        jnp.zeros((kv_heads, per_head, tokens_dev), jnp.float32),
    )


def shards(
    patches,
    route_count,
    text_states,
    segment_ids,
    vision_gain,
    merge_up,
    merge_down,
    norm_gain,
    query_weight,
    kv_weight,
):
    ctx_size = lax.axis_size("ctx")
    grp_size = lax.axis_size("grp")
    tp_size = lax.axis_size("tp")
    owner_index = lax.axis_index("ctx")
    member = lax.axis_index("grp")
    tp_index = lax.axis_index("tp")
    tensor_index = tp_index * grp_size + member
    row_count = patches.shape[0]
    bucket_rows = row_count // ctx_size
    tokens_dev = text_states.shape[0]
    grouped = patches.astype(jnp.float32).reshape(row_count, 4, -1)
    patch_normed = rms_scale(grouped, vision_gain).reshape(row_count, -1).astype(jnp.bfloat16)
    hidden = jax.nn.gelu(
        jnp.dot(patch_normed, merge_up, preferred_element_type=jnp.float32), approximate=False
    ).astype(jnp.bfloat16)
    partial_value = jnp.dot(hidden, merge_down, preferred_element_type=jnp.float32)
    column = lax.dynamic_slice_in_dim(route_count, owner_index, 1, 1)[:, 0]
    count_ends = jnp.cumsum(column)
    count_starts = count_ends - column
    slot_ids = jnp.arange(tokens_dev, dtype=jnp.int32)
    source = jnp.sum((count_ends[None, :] <= slot_ids[:, None]).astype(jnp.int32), axis=1)
    source = jnp.minimum(source, ctx_size - 1)
    source_match = source[:, None] == jnp.arange(ctx_size, dtype=jnp.int32)[None, :]
    first_slot = jnp.sum(jnp.where(source_match, count_starts[None, :], 0), axis=1)
    visual = slot_ids < count_ends[ctx_size - 1]
    pick_rows = jnp.where(visual, source * bucket_rows + slot_ids - first_slot, 0)
    merged = lax.psum(partial_value, ("tp", "grp")).astype(jnp.bfloat16)
    arrived = lax.all_to_all(
        merged.reshape(ctx_size, bucket_rows, -1), "ctx", split_axis=0, concat_axis=0, tiled=True
    )
    arrived = arrived.reshape(row_count, -1)
    text_full = lax.all_gather(text_states, ("tp", "grp"), axis=1, tiled=True)
    packed = jnp.where(visual[:, None], arrived[pick_rows], text_full)
    normal = rms_scale(packed.astype(jnp.float32), norm_gain).astype(jnp.bfloat16)
    queries = jnp.dot(normal, query_weight, preferred_element_type=jnp.float32).astype(jnp.bfloat16)
    kv_pairs = jnp.dot(normal, kv_weight, preferred_element_type=jnp.float32).astype(jnp.bfloat16)
    heads_dev = queries.shape[1] // HD
    group = HQ // KVH
    kv_per_tp = KVH // tp_size
    query_pos = owner_index * tokens_dev + slot_ids
    query_seg = segment_ids[query_pos]
    visual_count = jnp.sum(route_count, axis=0)
    kv_local = tensor_index * heads_dev // group - tp_index * kv_per_tp
    chosen = lax.dynamic_slice_in_dim(kv_pairs, kv_local * 2 * HD, 2 * HD, 1)
    queries4 = queries.reshape(tokens_dev, 1, heads_dev, HD)
    shard_piece = lax.all_gather(chosen, "ctx", axis=0, tiled=True)
    key_pos = jnp.arange(shard_piece.shape[0], dtype=jnp.int32)
    weighted, running_max, denominator = attend(
        start_state(1, heads_dev, tokens_dev),
        queries4,
        shard_piece,
        key_pos,
        query_pos,
        query_seg,
        segment_ids,
        visual_count,
        tokens_dev,
    )
    result = (weighted / denominator[..., None]).reshape(heads_dev, tokens_dev, HD)
    return result.transpose(1, 0, 2).reshape(tokens_dev, -1).astype(jnp.bfloat16)


def solution(mesh):
    return jax.shard_map(
        shards,
        mesh=mesh,
        in_specs=(
            P("ctx", None),
            P(),
            P("ctx", ("tp", "grp")),
            P(),
            P(),
            P(None, ("tp", "grp")),
            P(("tp", "grp"), None),
            P(),
            P(None, ("tp", "grp")),
            P(None, "tp"),
        ),
        out_specs=P("ctx", ("tp", "grp")),
        check_vma=False,
    )
```

profile of v0, /device:TPU:0, one launch (start us, length us, event | category | flops | bytes accessed | tf_op | source)
XLA Modules:
  0.0 106.3 jit_solution(12033060647353405200)
XLA Ops:
  6.5 1.0 convert_multiply_fusion.3
  7.7 0.7 mul.112
  8.5 4.6 %fusion.41 = f32[8,4096]{1,0:T(8,128)} fusion(bf16[320,4096]{1,0:T(8,128)(2,1)} %param.16, bf16[5120,320]{0,1:T(8,128)(2,1)S(1)} %copy-done, f32[8,5120]{1,0:T(8,128)S(1)} %bitcast.59, bf16[8,5120]{1,0:T(8,128)(2,1)} %param.10, f32[5120]{0:T(1024)S(1)} %mul.113), kind=kOutput, calls=%fused_computation.58 | convolution fusion | flops 47516160 | bytes 6295552 | tf_op jit(solution)/shard_map/dot_general | solution.py:96
  13.1 32.0 %all-reduce.1 = bf16[8,4096]{1,0:T(8,128)(2,1)S(1)} all-reduce(f32[8,4096]{1,0:T(8,128)} %fusion.41), channel_id=1, replica_groups=mesh['ctx'=4,'tp'=4,'grp'=2] {'tp','grp'}, use_global_device_ids=true, to_apply=%region_4.5 | all-reduce | flops 32768 | bytes 196608 | tf_op jit(solution)/shard_map/psum | solution.py:107
  45.8 3.7 %all-to-all-start = ((bf16[4,2,4096]{2,1,0:T(2,128)(2,1)}), bf16[4,2,4096]{2,1,0:T(2,128)(2,1)S(1)}, u32[]{:S(2)}, u32[]{:S(2)}) async-start(bf16[4,2,4096]{2,1,0:T(2,128)(2,1)} %reshape.183), calls=%async_computation | async-start | bytes 131072 | tf_op jit(solution)/shard_map/all_to_all | solution.py:108
  49.6 0.7 all-gather.2.cloned.1.call-update
  51.3 1.3 %gather_fusion = s32[128]{0:T(128)S(1)} fusion(s32[512]{0:T(512)S(1)} %copy-done.1, s32[1024]{0:T(1024)S(1)} %pad_clamp_fusion.1), kind=kCustom, calls=%fused_computation | custom fusion | bytes 1536 | tf_op jit(solution)/shard_map/gather | solution.py:121
  52.6 3.5 %gather_fusion.1 = s32[512]{0:T(512)S(1)} fusion(s32[512]{0:T(512)S(1)} %copy-done.1, s32[1024]{0:T(1024)S(1)} %pad_clamp_fusion), kind=kCustom, calls=%fused_computation.1 | custom fusion | bytes 6144 | tf_op jit(solution)/shard_map/gather | solution.py:39
  56.3 0.7 fusion.80
  57.1 0.8 fusion.19
  57.9 0.7 iota_compare_fusion.4
  58.7 2.2 %gather_fusion.2 = bf16[128,4096]{1,0:T(8,128)(2,1)} fusion(bf16[8,4096]{1,0:T(8,128)(2,1)S(1)} %reshape.184, s32[1024]{0:T(1024)S(1)} %pad_clamp_fusion.2), kind=kCustom, calls=%fused_computation.2 | custom fusion | bytes 2097664 | tf_op jit(solution)/shard_map/gather | solution.py:113
  60.9 12.1 %all-gather.2.cloned.1.call-done = bf16[128,4096]{1,0:T(8,128)(2,1)} async-done(((bf16[128,512]{1,0:T(8,128)(2,1)}), bf16[128,4096]{1,0:T(8,128)(2,1)}) %all-gather.2.cloned.1.call-update) | async-done | bytes 1048592 | tf_op jit(solution)/shard_map/all_gather | solution.py:112
  73.0 2.2 %fusion = (f32[128]{0:T(128)S(1)}, bf16[128,4096]{1,0:T(8,128)(2,1)S(1)}) fusion(bf16[128,4096]{1,0:T(8,128)(2,1)} %gather_fusion.2, bf16[128,4096]{1,0:T(8,128)(2,1)} %all-gather.2.cloned.1.call-done, pred[128]{0:T(512)(128)(4,1)S(1)} %iota_compare_fusion.4), kind=kLoop, calls=%fused_computation.5 | loop fusion | flops 2097024 | bytes 3146368 | tf_op jit(solution)/shard_map/reduce_sum | solution.py:14
  75.2 3.3 %fusion.16 = bf16[128,512]{1,0:T(8,128)(2,1)S(1)} fusion(bf16[4096,512]{1,0:T(8,128)(2,1)} %param.19, bf16[128,4096]{1,0:T(8,128)(2,1)S(1)} %get-tuple-element.6, f32[4096]{0:T(1024)S(1)} %copy-done.6, f32[128]{0:T(128)S(1)} %add_rsqrt_fusion.1), kind=kOutput, calls=%fused_computation.24 | convolution fusion | flops 538968064 | bytes 5390848 | tf_op jit(solution)/shard_map/dot_general | solution.py:116
  78.6 9.6 %all_gather.7 = bf16[512,256]{1,0:T(8,128)(2,1)} all-gather(bf16[128,256]{1,0:T(8,128)(2,1)S(1)} %dynamic-slice_convert_fusion), channel_id=1, replica_groups=mesh['ctx'=4,'tp'=4,'grp'=2] {'ctx'}, dimensions={0}, use_global_device_ids=true | all-gather | bytes 327680 | tf_op jit(solution)/shard_map/all_gather | solution.py:126
  88.2 1.0 reshape.185
  89.2 1.1 %fusion.113 = (bf16[512,1,1,128]{3,2,0,1:T(2,128)(2,1)}, bf16[512,1,1,128]{3,2,0,1:T(2,128)(2,1)S(1)}) fusion(bf16[512,1,2,128]{3,2,0,1:T(2,128)(2,1)S(1)} %reshape.185), kind=kLoop, calls=%fused_computation.155 | loop fusion | bytes 524288 | tf_op jit(solution)/shard_map/slice | solution.py:34
  90.3 3.3 %fusion.7 = bf16[16,4,8,128]{3,2,1,0:T(8,128)(2,1)S(1)} fusion(bf16[4096,512]{1,0:T(8,128)(2,1)} %param.18, bf16[128,4096]{1,0:T(8,128)(2,1)} %copy-done.2, f32[4096]{0:T(1024)S(1)} %copy-done.6, f32[128]{0:T(128)} %copy-done.7), kind=kOutput, calls=%fused_computation.15 | convolution fusion | flops 539033600 | bytes 5390848 | tf_op jit(solution)/shard_map/dot_general | solution.py:115
  93.6 1.3 %fusion.114 = (f32[4,128]{1,0:T(4,128)S(1)}, f32[1,4,128,512]{2,3,1,0:T(8,128)}) fusion(bf16[16,4,8,128]{3,2,1,0:T(8,128)(2,1)S(1)} %fusion.7, bf16[512,1,1,128]{3,2,0,1:T(2,128)(2,1)S(1)} %get-tuple-element.10, pred[128,512]{0,1:T(8,128)(4,1)S(1)} %copy-done.4), kind=kOutput, calls=%fused_computation.156 | convolution fusion | flops 67894784 | bytes 1378304 | tf_op jit(solution)/shard_map/qkgd,rkd->kgqr/dot_general | solution.py:45
  94.9 0.8 copy.27
  95.7 1.4 %fusion.8 = f32[4,128]{1,0:T(4,128)S(1)} fusion(f32[1,4,128,512]{2,3,1,0:T(8,128)} %get-tuple-element.12, f32[4,128]{1,0:T(4,128)S(1)} %broadcast_maximum_fusion, pred[128,512]{0,1:T(8,128)(4,1)} %fusion.19), kind=kLoop, calls=%fused_computation.18 | loop fusion | flops 785920 | bytes 1118208 | tf_op jit(solution)/shard_map/reduce_sum | solution.py:51
  97.1 1.6 %fusion.6 = bf16[128,4,128]{0,2,1:T(8,128)(2,1)S(1)} fusion(f32[1,4,128,512]{2,3,1,0:T(8,128)} %get-tuple-element.12, f32[4,128]{1,0:T(4,128)S(1)} %broadcast_maximum_fusion, pred[128,512]{0,1:T(8,128)(4,1)} %fusion.19, bf16[512,1,1,128]{0,3,2,1:T(8,128)(2,1)} %copy.27, f32[128,4]{0,1:T(4,128)S(1)} %bitcast.62), kind=kOutput, calls=%fused_computation.13 | convolution fusion | flops 68026368 | bytes 1380352 | tf_op jit(solution)/shard_map/kgqr,rkd->kgqd/dot_general | solution.py:52
  98.7 0.8 copy.25
  (45 shorter events, 2.3 us)
Async XLA Ops:
  6.5 2.0 %copy-start = (bf16[5120,320]{0,1:T(8,128)(2,1)S(1)}, bf16[5120,320]{0,1:T(8,128)(2,1)}, u32[]{:S(2)}) copy-start(bf16[5120,320]{0,1:T(8,128)(2,1)} %param.15) | copy-start | bytes 9830404
  8.5 41.8 %copy-start.5 = (s32[4,4]{1,0:T(4,128)S(1)}, s32[4,4]{1,0:T(4,128)}, u32[]{:S(2)}) copy-start(s32[4,4]{1,0:T(4,128)} %param.11) | copy-start | bytes 196
  8.5 42.8 %copy-start.1 = (s32[512]{0:T(512)S(1)}, s32[512]{0:T(512)}, u32[]{:S(2)}) copy-start(s32[512]{0:T(512)} %param.13) | copy-start | bytes 6148
  45.8 12.8 %all-to-all-start = ((bf16[4,2,4096]{2,1,0:T(2,128)(2,1)}), bf16[4,2,4096]{2,1,0:T(2,128)(2,1)S(1)}, u32[]{:S(2)}, u32[]{:S(2)}) async-start(bf16[4,2,4096]{2,1,0:T(2,128)(2,1)} %reshape.183), calls=%async_computation | async-start | bytes 131072 | tf_op jit(solution)/shard_map/all_to_all | solution.py:108
  49.6 23.5 %all-gather.2.cloned.1.call-start = ((), (), s32[]{:S(2)}) async-start(), calls=%async_computation.1 | async-start | bytes 1179648 | tf_op jit(solution)/shard_map/all_gather | solution.py:112
  60.9 14.3 %copy-start.6 = (f32[4096]{0:T(1024)S(1)}, f32[4096]{0:T(1024)}, u32[]{:S(2)}) copy-start(f32[4096]{0:T(1024)} %param.17) | copy-start | bytes 49156
  75.2 3.4 %copy-start.2 = (bf16[128,4096]{1,0:T(8,128)(2,1)}, bf16[128,4096]{1,0:T(8,128)(2,1)S(1)}, u32[]{:S(2)}) copy-start(bf16[128,4096]{1,0:T(8,128)(2,1)S(1)} %get-tuple-element.6) | copy-start | bytes 3145732
  75.2 3.4 %copy-start.7 = (f32[128]{0:T(128)}, f32[128]{0:T(128)S(1)}, u32[]{:S(2)}) copy-start(f32[128]{0:T(128)S(1)} %add_rsqrt_fusion.1) | copy-start | bytes 1540
  90.3 3.3 %copy-start.4 = (pred[128,512]{0,1:T(8,128)(4,1)S(1)}, pred[128,512]{0,1:T(8,128)(4,1)}, u32[]{:S(2)}) copy-start(pred[128,512]{0,1:T(8,128)(4,1)} %fusion.19) | copy-start | bytes 196612
  90.3 4.6 %copy-start.3 = (bf16[512,1,1,128]{3,2,0,1:T(2,128)(2,1)S(1)}, bf16[512,1,1,128]{3,2,0,1:T(2,128)(2,1)}, u32[]{:S(2)}) copy-start(bf16[512,1,1,128]{3,2,0,1:T(2,128)(2,1)} %get-tuple-element.9) | copy-start | bytes 393220
Sparse Core Ops, SparseCore 0:
  52.0 21.0 all-gather.1
where the time goes:
time: 107 us; the launch traced here: 106 us
  blocking collectives  41.6 us (39%)
  matrix products  14.1 us (13%)
  between operations  13.7 us (13%)
  local copies, waits for them, and re-layouts  13 us (12%)
  waiting for transfers between devices  12.8 us (12%)
  other arithmetic  7.46 us (7%)
  starting transfers between devices  3.72 us (3%)
    psum x1, blocking collectives, shards(): merged = lax.psum(partial_value, ('tp', 'grp')).astype(jnp.bfloat16)  32 us
    all_gather x1, waiting for transfers between devices, shards(): text_full = lax.all_gather(text_states, ('tp', 'grp'), axis=1, tiled=True)  12.1 us
    all_gather x1, blocking collectives, shards(): shard_piece = lax.all_gather(chosen, 'ctx', axis=0, tiled=True)  9.55 us
    dot_general x1, matrix products, shards(): jnp.dot(hidden, merge_down, preferred_element_type=jnp.float32)  4.57 us
    all_to_all x1, starting transfers between devices, shards(): lax.all_to_all(merged.reshape(ctx_size, bucket_rows, -1), 'ctx', split_ax...  3.72 us
    gather x1, local copies, waits for them, and re-layouts, attend(): key_seg = segment_ids[key_pos]  3.49 us
    dot_general x1, matrix products, shards(): jnp.dot(normal, kv_weight, preferred_element_type=jnp.float32)  3.34 us
    dot_general x1, matrix products, shards(): jnp.dot(normal, query_weight, preferred_element_type=jnp.float32)  3.32 us
  transfers between devices with their start and end apart: 2, of which 1 were waited for; matrix products, arithmetic and copies ran while one was open for 10% of the time, Pallas kernels for 0%

commit v1 on v0

--- a/solution.py
+++ b/solution.py
@@ -8,6 +8,16 @@
 HD = 128
 EPSILON = 1e-06
 NEGATIVE = -1e30
+
+
+def gather_by_hops(x, mesh_axis, dim):
+    size = lax.axis_size(mesh_axis)
+    held, blocks = (x, [x])
+    for _ in range(size - 1):
+        held = lax.ppermute(held, mesh_axis, [(i, (i + 1) % size) for i in range(size)])
+        blocks.insert(0, held)
+    line = jnp.concatenate(blocks, axis=dim)
+    return jnp.roll(line, (lax.axis_index(mesh_axis) + 1) * x.shape[dim], axis=dim)
 
 
 def rms_scale(values, gain):
@@ -123,7 +133,7 @@
     kv_local = tensor_index * heads_dev // group - tp_index * kv_per_tp
     chosen = lax.dynamic_slice_in_dim(kv_pairs, kv_local * 2 * HD, 2 * HD, 1)
     queries4 = queries.reshape(tokens_dev, 1, heads_dev, HD)
-    shard_piece = lax.all_gather(chosen, "ctx", axis=0, tiled=True)
+    shard_piece = gather_by_hops(chosen, "ctx", 0)
     key_pos = jnp.arange(shard_piece.shape[0], dtype=jnp.int32)
     weighted, running_max, denominator = attend(
         start_state(1, heads_dev, tokens_dev),

time: 107 us -> 95.1 us (0.89)
  blocking collectives: 41.6 us -> 33.1 us
  waiting for transfers between devices: 12.8 us -> 8.07 us
  starting transfers between devices: 3.72 us -> 7.08 us
  local copies, waits for them, and re-layouts: 13 us -> 11 us
    all_gather x1, waiting for transfers between devices: 12.1 us -> 0.01 us  [shards(): text_full = lax.all_gather(text_states, ('tp', 'grp'), axis=1, tiled=True)]
    all_gather x1 -> x0, blocking collectives: 9.55 us -> none  [shards(): shard_piece = lax.all_gather(chosen, 'ctx', axis=0, tiled=True)]
    ppermute x0 -> x3, waiting for transfers between devices: none -> 7.35 us  [gather_by_hops(): lax.ppermute(held, mesh_axis, [(i, (i + 1) % size) for i in range(size)])]
    ppermute x0 -> x3, starting transfers between devices: none -> 3.42 us  [gather_by_hops(): lax.ppermute(held, mesh_axis, [(i, (i + 1) % size) for i in range(size)])]
    slice x1 -> x0, local copies, waits for them, and re-layouts: 1.08 us -> none  [attend(): value_block = kv_split[:, :, 1]]
  transfers between devices with their start and end apart: 2 -> 5, of which waited for: 1 -> 3; matrix products, arithmetic and copies ran while one was open for 10% -> 23% of each run, Pallas kernels for 0% -> 0%
where the time goes in v1:
time: 95.1 us; the launch traced here: 94.6 us
  blocking collectives  33.1 us (35%)
  matrix products  14.4 us (15%)
  between operations  13.7 us (14%)
  local copies, waits for them, and re-layouts  11 us (12%)
  waiting for transfers between devices  8.07 us (8%)
  other arithmetic  7.19 us (8%)
  starting transfers between devices  7.08 us (7%)
    psum x1, blocking collectives, shards(): merged = lax.psum(partial_value, ('tp', 'grp')).astype(jnp.bfloat16)  33.1 us
    ppermute x3, waiting for transfers between devices, gather_by_hops(): lax.ppermute(held, mesh_axis, [(i, (i + 1) % size) for i in range(size)])  7.35 us
    dot_general x1, matrix products, shards(): jnp.dot(hidden, merge_down, preferred_element_type=jnp.float32)  4.57 us
    dot_general x1, matrix products, shards(): jnp.dot(normal, query_weight, preferred_element_type=jnp.float32)  3.95 us
    all_to_all x1, starting transfers between devices, shards(): lax.all_to_all(merged.reshape(ctx_size, bucket_rows, -1), 'ctx', split_ax...  3.65 us
    gather x1, local copies, waits for them, and re-layouts, attend(): key_seg = segment_ids[key_pos]  3.49 us
    ppermute x3, starting transfers between devices, gather_by_hops(): lax.ppermute(held, mesh_axis, [(i, (i + 1) % size) for i in range(size)])  3.42 us
    dot_general x1, matrix products, shards(): jnp.dot(normal, kv_weight, preferred_element_type=jnp.float32)  3.37 us
  transfers between devices with their start and end apart: 5, of which 3 were waited for; matrix products, arithmetic and copies ran while one was open for 23% of the time, Pallas kernels for 0%

profile of v1, /device:TPU:0, one launch (start us, length us, event | category | flops | bytes accessed | tf_op | source)
XLA Modules:
  0.0 94.6 jit_solution(17619007170367978745)
XLA Ops:
  6.5 0.7 all-gather.2.cloned.1.call-update
  7.3 1.2 %convert_multiply_fusion.3 = f32[8,5120]{1,0:T(8,128)S(1)} fusion(bf16[8,5120]{1,0:T(8,128)(2,1)} %param.10), kind=kLoop, calls=%fused_computation.29 | loop fusion | flops 81920 | bytes 245760 | tf_op jit(solution)/shard_map/mul | solution.py:24
  8.5 0.7 mul.115
  9.4 4.6 %fusion.40 = f32[8,4096]{1,0:T(8,128)} fusion(bf16[320,4096]{1,0:T(8,128)(2,1)} %param.16, bf16[5120,320]{0,1:T(8,128)(2,1)S(1)} %copy-done, f32[8,5120]{1,0:T(8,128)S(1)} %bitcast.61, bf16[8,5120]{1,0:T(8,128)(2,1)} %param.10, f32[5120]{0:T(1024)S(1)} %mul.116), kind=kOutput, calls=%fused_computation.66 | convolution fusion | flops 47516160 | bytes 6295552 | tf_op jit(solution)/shard_map/dot_general | solution.py:106
  13.9 33.1 %all-reduce.1 = bf16[8,4096]{1,0:T(8,128)(2,1)S(1)} all-reduce(f32[8,4096]{1,0:T(8,128)} %fusion.40), channel_id=1, replica_groups=mesh['ctx'=4,'tp'=4,'grp'=2] {'tp','grp'}, use_global_device_ids=true, to_apply=%region_4.5 | all-reduce | flops 32768 | bytes 196608 | tf_op jit(solution)/shard_map/psum | solution.py:117
  47.7 3.7 %all-to-all-start = ((bf16[4,2,4096]{2,1,0:T(2,128)(2,1)}), bf16[4,2,4096]{2,1,0:T(2,128)(2,1)S(1)}, u32[]{:S(2)}, u32[]{:S(2)}) async-start(bf16[4,2,4096]{2,1,0:T(2,128)(2,1)} %reshape.183), calls=%async_computation | async-start | bytes 131072 | tf_op jit(solution)/shard_map/all_to_all | solution.py:118
  52.5 0.7 fusion.79
  54.1 1.3 %gather_fusion = s32[128]{0:T(128)S(1)} fusion(s32[512]{0:T(512)S(1)} %copy-done.1, s32[1024]{0:T(1024)S(1)} %pad_clamp_fusion.1), kind=kCustom, calls=%fused_computation | custom fusion | bytes 1536 | tf_op jit(solution)/shard_map/gather | solution.py:131
  55.4 3.5 %gather_fusion.1 = s32[512]{0:T(512)S(1)} fusion(s32[512]{0:T(512)S(1)} %copy-done.1, s32[1024]{0:T(1024)S(1)} %pad_clamp_fusion), kind=kCustom, calls=%fused_computation.1 | custom fusion | bytes 6144 | tf_op jit(solution)/shard_map/gather | solution.py:49
  58.9 2.2 %gather_fusion.2 = bf16[128,4096]{1,0:T(8,128)(2,1)} fusion(bf16[8,4096]{1,0:T(8,128)(2,1)S(1)} %reshape.184, s32[1024]{0:T(1024)S(1)} %pad_clamp_fusion.2), kind=kCustom, calls=%fused_computation.2 | custom fusion | bytes 2097664 | tf_op jit(solution)/shard_map/gather | solution.py:123
  61.2 2.2 %fusion = (f32[128]{0:T(128)S(1)}, bf16[128,4096]{1,0:T(8,128)(2,1)S(1)}) fusion(bf16[128,4096]{1,0:T(8,128)(2,1)} %gather_fusion.2, bf16[128,4096]{1,0:T(8,128)(2,1)} %all-gather.2.cloned.1.call-done, pred[128]{0:T(512)(128)(4,1)S(1)} %iota_compare_fusion.4), kind=kLoop, calls=%fused_computation.5 | loop fusion | flops 2097024 | bytes 3146368 | tf_op jit(solution)/shard_map/reduce_sum | solution.py:24
  63.4 3.4 %fusion.16 = bf16[128,512]{1,0:T(8,128)(2,1)S(1)} fusion(bf16[4096,512]{1,0:T(8,128)(2,1)} %param.19, bf16[128,4096]{1,0:T(8,128)(2,1)S(1)} %get-tuple-element.6, f32[4096]{0:T(1024)S(1)} %copy-done.4, f32[128]{0:T(128)S(1)} %add_rsqrt_fusion.1), kind=kOutput, calls=%fused_computation.24 | convolution fusion | flops 538968064 | bytes 5390848 | tf_op jit(solution)/shard_map/dot_general | solution.py:126
  66.8 2.1 %collective-permute-start = (bf16[128,256]{1,0:T(8,128)(2,1)S(1)}, bf16[128,256]{1,0:T(8,128)(2,1)S(1)}, u32[]{:S(2)}, u32[]{:S(2)}) collective-permute-start(bf16[128,256]{1,0:T(8,128)(2,1)S(1)} %dynamic-slice_convert_fusion), channel_id=1, source_target_pairs={{0,8},{8,16},{16,24},{24,0},{1,9},{9,17},{17,25},{25,1},{2,10},{10... | collective-permute-start | bytes 196616 | tf_op jit(solution)/shard_map/ppermute | solution.py:17
  68.9 3.1 %collective-permute-done = bf16[128,256]{1,0:T(8,128)(2,1)S(1)} collective-permute-done((bf16[128,256]{1,0:T(8,128)(2,1)S(1)}, bf16[128,256]{1,0:T(8,128)(2,1)S(1)}, u32[]{:S(2)}, u32[]{:S(2)}) %collective-permute-start) | collective-permute-done | bytes 65568 | tf_op jit(solution)/shard_map/ppermute | solution.py:17
  72.0 1.1 %collective-permute-start.1 = (bf16[128,256]{1,0:T(8,128)(2,1)S(1)}, bf16[128,256]{1,0:T(8,128)(2,1)S(1)}, u32[]{:S(2)}, u32[]{:S(2)}) collective-permute-start(bf16[128,256]{1,0:T(8,128)(2,1)S(1)} %collective-permute-done), channel_id=1, source_target_pairs={{0,8},{8,16},{16,24},{24,0},{1,9},{9,17},{17,25},{25,1},{2,10},{10... | collective-permute-start | bytes 196616 | tf_op jit(solution)/shard_map/ppermute | solution.py:17
  73.1 0.8 fusion.19
  74.0 3.2 %collective-permute-done.1 = bf16[128,256]{1,0:T(8,128)(2,1)S(1)} collective-permute-done((bf16[128,256]{1,0:T(8,128)(2,1)S(1)}, bf16[128,256]{1,0:T(8,128)(2,1)S(1)}, u32[]{:S(2)}, u32[]{:S(2)}) %collective-permute-start.1) | collective-permute-done | bytes 65568 | tf_op jit(solution)/shard_map/ppermute | solution.py:17
  77.4 3.9 %fusion.7 = bf16[16,4,8,128]{3,2,1,0:T(8,128)(2,1)} fusion(bf16[4096,512]{1,0:T(8,128)(2,1)} %param.18, bf16[128,4096]{1,0:T(8,128)(2,1)} %copy-done.2, f32[4096]{0:T(1024)} %param.17, f32[128]{0:T(128)S(1)} %add_rsqrt_fusion.1), kind=kOutput, calls=%fused_computation.15 | convolution fusion | flops 539033600 | bytes 5390848 | tf_op jit(solution)/shard_map/dot_general | solution.py:125
  81.3 1.0 %collective-permute-done.2 = bf16[128,256]{1,0:T(8,128)(2,1)S(1)} collective-permute-done((bf16[128,256]{1,0:T(8,128)(2,1)S(1)}, bf16[128,256]{1,0:T(8,128)(2,1)S(1)}, u32[]{:S(2)}, u32[]{:S(2)}) %collective-permute-start.2) | collective-permute-done | bytes 65568 | tf_op jit(solution)/shard_map/ppermute | solution.py:17
  82.5 0.8 copy.20
  83.3 1.3 %fusion.112 = (f32[4,128]{1,0:T(4,128)S(1)}, f32[1,4,128,512]{2,3,1,0:T(8,128)S(1)}) fusion(bf16[16,4,8,128]{3,2,1,0:T(8,128)(2,1)} %fusion.7, bf16[512,1,2,128]{0,3,2,1:T(8,128)(2,1)} %bitcast.63, pred[128,512]{0,1:T(8,128)(4,1)} %fusion.19), kind=kOutput, calls=%fused_computation.164 | convolution fusion | flops 67894784 | bytes 1378304 | tf_op jit(solution)/shard_map/qkgd,rkd->kgqr/dot_general | solution.py:55
  84.6 1.0 %fusion.8 = f32[4,128]{1,0:T(4,128)S(1)} fusion(f32[1,4,128,512]{2,3,1,0:T(8,128)S(1)} %get-tuple-element.10, f32[4,128]{1,0:T(4,128)S(1)} %broadcast_maximum_fusion, pred[128,512]{0,1:T(8,128)(4,1)} %fusion.19), kind=kLoop, calls=%fused_computation.18 | loop fusion | flops 785920 | bytes 1118208 | tf_op jit(solution)/shard_map/reduce_sum | solution.py:61
  85.7 1.3 %fusion.6 = bf16[128,4,128]{0,2,1:T(8,128)(2,1)S(1)} fusion(f32[1,4,128,512]{2,3,1,0:T(8,128)S(1)} %get-tuple-element.10, f32[4,128]{1,0:T(4,128)S(1)} %broadcast_maximum_fusion, pred[128,512]{0,1:T(8,128)(4,1)} %fusion.19, bf16[512,1,2,128]{0,3,2,1:T(8,128)(2,1)} %bitcast.64, f32[128,4]{0,1:T(4,128)S(1)} %bitcast.66), kind=kOutput, calls=%fused_computation.13 | convolution fusion | flops 68026368 | bytes 1380352 | tf_op jit(solution)/shard_map/kgqr,rkd->kgqd/dot_general | solution.py:62
  87.0 0.8 copy.24
  (51 shorter events, 3.2 us)
Async XLA Ops:
  6.5 2.8 %copy-start = (bf16[5120,320]{0,1:T(8,128)(2,1)S(1)}, bf16[5120,320]{0,1:T(8,128)(2,1)}, u32[]{:S(2)}) copy-start(bf16[5120,320]{0,1:T(8,128)(2,1)} %param.15) | copy-start | bytes 9830404
  6.5 54.6 %all-gather.2.cloned.1.call-start = ((), (), s32[]{:S(2)}) async-start(), calls=%async_computation.1 | async-start | bytes 1179648 | tf_op jit(solution)/shard_map/all_gather | solution.py:122
  9.3 42.0 %copy-start.3 = (s32[4,4]{1,0:T(4,128)S(1)}, s32[4,4]{1,0:T(4,128)}, u32[]{:S(2)}) copy-start(s32[4,4]{1,0:T(4,128)} %param.11) | copy-start | bytes 196
  9.4 44.8 %copy-start.1 = (s32[512]{0:T(512)S(1)}, s32[512]{0:T(512)}, u32[]{:S(2)}) copy-start(s32[512]{0:T(512)} %param.13) | copy-start | bytes 6148
  47.7 11.2 %all-to-all-start = ((bf16[4,2,4096]{2,1,0:T(2,128)(2,1)}), bf16[4,2,4096]{2,1,0:T(2,128)(2,1)S(1)}, u32[]{:S(2)}, u32[]{:S(2)}) async-start(bf16[4,2,4096]{2,1,0:T(2,128)(2,1)} %reshape.183), calls=%async_computation | async-start | bytes 131072 | tf_op jit(solution)/shard_map/all_to_all | solution.py:118
  61.2 2.2 %copy-start.4 = (f32[4096]{0:T(1024)S(1)}, f32[4096]{0:T(1024)}, u32[]{:S(2)}) copy-start(f32[4096]{0:T(1024)} %param.17) | copy-start | bytes 49156
  63.3 3.4 %copy-start.2 = (bf16[128,4096]{1,0:T(8,128)(2,1)}, bf16[128,4096]{1,0:T(8,128)(2,1)S(1)}, u32[]{:S(2)}) copy-start(bf16[128,4096]{1,0:T(8,128)(2,1)S(1)} %get-tuple-element.6) | copy-start | bytes 3145732
  66.8 5.2 %collective-permute-start = (bf16[128,256]{1,0:T(8,128)(2,1)S(1)}, bf16[128,256]{1,0:T(8,128)(2,1)S(1)}, u32[]{:S(2)}, u32[]{:S(2)}) collective-permute-start(bf16[128,256]{1,0:T(8,128)(2,1)S(1)} %dynamic-slice_convert_fusion), channel_id=1, source_target_pairs={{0,8},{8,16},{16,24},{24,0},{1,9},{9,17},{17,25},{25,1},{2,10},{10... | collective-permute-start | bytes 196616 | tf_op jit(solution)/shard_map/ppermute | solution.py:17
  72.0 5.2 %collective-permute-start.1 = (bf16[128,256]{1,0:T(8,128)(2,1)S(1)}, bf16[128,256]{1,0:T(8,128)(2,1)S(1)}, u32[]{:S(2)}, u32[]{:S(2)}) collective-permute-start(bf16[128,256]{1,0:T(8,128)(2,1)S(1)} %collective-permute-done), channel_id=1, source_target_pairs={{0,8},{8,16},{16,24},{24,0},{1,9},{9,17},{17,25},{25,1},{2,10},{10... | collective-permute-start | bytes 196616 | tf_op jit(solution)/shard_map/ppermute | solution.py:17
  77.2 5.2 %collective-permute-start.2 = (bf16[128,256]{1,0:T(8,128)(2,1)S(1)}, bf16[128,256]{1,0:T(8,128)(2,1)S(1)}, u32[]{:S(2)}, u32[]{:S(2)}) collective-permute-start(bf16[128,256]{1,0:T(8,128)(2,1)S(1)} %collective-permute-done.1), channel_id=1, source_target_pairs={{0,8},{8,16},{16,24},{24,0},{1,9},{9,17},{17,25},{25,1},{2,10},{10... | collective-permute-start | bytes 196616 | tf_op jit(solution)/shard_map/ppermute | solution.py:17
Sparse Core Ops, SparseCore 0:
  8.9 25.5 all-gather.1
